TPU v7x, 32 devices: a whole 2x2x4 slice. The times are simulated.
32 devices in a mesh: member: 2 (over x), space: 16 (over z, y, core).
Axes of the slice: x: 2, y: 2, z: 4, core: 2. Of those that a mesh axis runs over, the one named last changes fastest.
Arguments:
- node_states: bfloat16 [4096, 1024], P('space'), may hold values from -6 to 6
- noise: bfloat16 [2, 16, 4096], P('member', None, 'space'), may hold values from -4 to 4
- norm_gain: float32 [1024], replicated, may hold values from 0.5 to 1.5
- cond_weight: bfloat16 [16, 2048], replicated, may hold values from -1.5 to 1.5
- w_query: bfloat16 [1024, 1024], P('space'), may hold values from -0.1875 to 0.1875
- w_key: bfloat16 [1024, 1024], P('space'), may hold values from -0.1875 to 0.1875
- w_value: bfloat16 [1024, 1024], P('space'), may hold values from -0.1875 to 0.1875
- w_out: bfloat16 [1024, 1024], P('space'), may hold values from -0.1875 to 0.1875
- edge_src: int32 [8, 4096], P(None, 'space'), may hold values from 0 to 511, as said below
- send_rows: int32 [4096], P('space'), may hold values from 0 to 255, as said below
- dec_src: int32 [3, 16384], P(None, 'space'), may hold values from 0 to 255
- dec_weight: float32 [3, 16384], P(None, 'space'), may hold values from 0.2 to 1
- w_decode: bfloat16 [100, 1024], replicated, may hold values from -0.1875 to 0.1875
- truth: bfloat16 [100, 16384], P(None, 'space'), may hold values from -6 to 6
- area: float32 [16384], P('space'), may hold values from 0.1 to 3.5
Outputs:
- loss: float32 [], replicated
- field_grad: bfloat16 [2, 100, 16384], P('member', None, 'space')
Inputs may be any that keep to these rules, and one draw needn't show every extreme that they name: `send_rows`: each block's 2 * 128 entries are distinct node indices within that block. `edge_src`: entries below 128 name a row of the previous block's halo rows, entries from 384 on a row of the next block's; of each such halo half only a leading part of at least 64 rows is named, its length varying by block, and in some block the whole half is named.
All inputs are finite; a program needn't handle non-finite values.
Results may differ from a plain program's by a relative error of at most 0.015.
Values may be sent and summed in bfloat16 or wider, within the bound.
No kernel may reach another device: no remote copies, remote signals or barrier semaphores. Data moves between devices by JAX's collectives and lax.ppermute only.
A program may use at most 64 MiB of HBM per device.

v0:
```python
import jax
import jax.numpy as jnp
from jax import lax
from jax.sharding import PartitionSpec as P

HEADS = 16


SMOOTH = 0.25
EPS = 1e-05


def extended(block, sides, width):
    for axis, dim in sides:
        count = lax.axis_size(axis)
        forward = [(i, i + 1) for i in range(count - 1)]
        forward.append((count - 1, 0))
        backward = [(target, source) for source, target in forward]
        low = lax.ppermute(
            lax.slice_in_dim(block, block.shape[dim] - width, None, axis=dim), axis, forward
        )
        high = lax.ppermute(lax.slice_in_dim(block, 0, width, axis=dim), axis, backward)
        block = jnp.concatenate([low, block, high], axis=dim)
    return block


def condition(states, noise_block, norm_gain, cond_weight):
    values = states.astype(jnp.float32)
    center = values - jnp.mean(values, axis=1, keepdims=True)
    spread = jnp.mean(center * center, axis=1, keepdims=True)
    normed = center * lax.rsqrt(spread + EPS)
    terms = lax.dot_general(
        noise_block, cond_weight, (((0,), (0,)), ((), ())), preferred_element_type=jnp.float32
    )
    model_width = states.shape[1]
    return (normed * norm_gain * (1.0 + terms[:, :model_width]) + terms[:, model_width:]).astype(
        jnp.bfloat16
    )


def attention(query_rows, key_ext, value_ext, sources):
    row_count, model_width = query_rows.shape
    head_size = model_width // HEADS
    factor = 1.0 / head_size**0.5
    query_wide = query_rows.astype(jnp.float32).reshape(row_count, HEADS, head_size)
    numerator = jnp.zeros((row_count, HEADS, head_size), jnp.float32)
    denominator = jnp.zeros((row_count, HEADS), jnp.float32)
    for slot_index in range(sources.shape[0]):
        picked = sources[slot_index]
        gathered_key = key_ext[picked].astype(jnp.float32).reshape(row_count, HEADS, head_size)
        weight = jnp.exp(jnp.sum(query_wide * gathered_key, axis=2) * factor)
        gathered_value = value_ext[picked].astype(jnp.float32).reshape(row_count, HEADS, head_size)
        numerator = numerator + weight[:, :, None] * gathered_value
        denominator = denominator + weight
    return (
        (numerator / denominator[:, :, None]).reshape(row_count, model_width).astype(jnp.bfloat16)
    )


def decode(processed, sources, dec_weight, w_decode):
    gathered = jnp.zeros((sources.shape[1], processed.shape[1]), jnp.float32)
    for neighbour in range(sources.shape[0]):
        gathered = gathered + dec_weight[neighbour][:, None] * processed[sources[neighbour]].astype(
            jnp.float32
        )
    return lax.dot_general(
        w_decode,
        gathered.astype(jnp.bfloat16),
        (((1,), (1,)), ((), ())),
        preferred_element_type=jnp.float32,
    ).astype(jnp.bfloat16)


def smooth_abs(difference):
    return jnp.sqrt(difference * difference + SMOOTH * SMOOTH)


def per_device(
    node_states,
    noise,
    norm_gain,
    cond_weight,
    w_query,
    w_key,
    w_value,
    w_out,
    edge_src,
    send_rows,
    dec_src,
    dec_weight,
    w_decode,
    truth,
    area,
):
    hidden = condition(node_states, noise[0], norm_gain, cond_weight)
    halo_rows = send_rows.shape[0] // 2
    padded = extended(hidden[send_rows], (("space", 0),), halo_rows)
    kv_input = jnp.concatenate((padded[:halo_rows], hidden, padded[3 * halo_rows :]), axis=0)
    whole_query, whole_key, whole_value = (
        lax.all_gather(w_query, "space", axis=0, tiled=True),
        lax.all_gather(w_key, "space", axis=0, tiled=True),
        lax.all_gather(w_value, "space", axis=0, tiled=True),
    )
    query_rows = jnp.dot(hidden, whole_query, preferred_element_type=jnp.float32).astype(
        jnp.bfloat16
    )
    key_rows = jnp.dot(kv_input, whole_key, preferred_element_type=jnp.float32).astype(jnp.bfloat16)
    value_rows = jnp.dot(kv_input, whole_value, preferred_element_type=jnp.float32).astype(
        jnp.bfloat16
    )
    key_ext, value_ext = (key_rows, value_rows)
    attended = attention(query_rows, key_ext, value_ext, edge_src)
    whole_out = lax.all_gather(w_out, "space", axis=0, tiled=True)
    update = jnp.dot(attended, whole_out, preferred_element_type=jnp.float32)
    processed = (node_states.astype(jnp.float32) + update).astype(jnp.bfloat16)
    fields = decode(processed, dec_src, dec_weight, w_decode)
    truth_wide = truth.astype(jnp.float32)
    members = lax.axis_size("member")
    pair_norm = 2.0 * members * (members - 1)
    columns = fields.shape[1] // members
    offset = lax.axis_index("member") * columns
    all_fields = lax.all_gather(fields[None], "member", axis=0, tiled=True)
    every_value = all_fields.astype(jnp.float32)
    own_values = fields.astype(jnp.float32)
    skill_gap = own_values - truth_wide
    skill_abs = smooth_abs(skill_gap)
    spread_slope = jnp.zeros_like(own_values)
    for other_member in range(members):
        difference = own_values - every_value[other_member]
        spread_slope = spread_slope + difference / smooth_abs(difference)
    field_grad = (area[None, :] * (skill_gap / skill_abs - spread_slope / (members - 1))).astype(
        jnp.bfloat16
    )[None]
    part_values = lax.dynamic_slice_in_dim(every_value, offset, columns, 2)
    truth_part = lax.dynamic_slice_in_dim(truth_wide, offset, columns, 1)
    area_part = lax.dynamic_slice_in_dim(area, offset, columns, 0)
    part_skill = smooth_abs(part_values - truth_part[None])
    part_spread = jnp.zeros_like(part_values)
    for other_member in range(members):
        part_spread = part_spread + smooth_abs(part_values - part_values[other_member][None])
    crps_value = (
        jnp.sum(part_skill, axis=0) / members
        - (jnp.sum(part_spread, axis=0) - members * SMOOTH) / pair_norm
    )
    local_sum = jnp.sum(area_part[None, :] * crps_value)
    loss_sum = lax.psum(local_sum, ("member", "space"))
    loss = loss_sum / (truth.shape[0] * truth.shape[1] * lax.axis_size("space"))
    return (loss, field_grad)


def solution(mesh):
    in_specs = (
        P("space", None),
        P("member", None, "space"),
        P(),
        P(),
        P("space", None),
        P("space", None),
        P("space", None),
        P("space", None),
        P(None, "space"),
        P("space"),
        P(None, "space"),
        P(None, "space"),
        P(),
        P(None, "space"),
        P("space"),
    )
    out_specs = (P(), P("member", None, "space"))
    return jax.shard_map(
        per_device, mesh=mesh, in_specs=in_specs, out_specs=out_specs, check_vma=False
    )
```

profile of v0, /device:TPU:0, one launch (start us, length us, event | category | flops | bytes accessed | tf_op | source)
XLA Modules:
  0.0 282.5 jit_solution(3880924004509811055)
XLA Ops:
  16.2 5.0 %collective-permute-start.1 = (bf16[128,1024]{1,0:T(8,128)(2,1)S(1)}, bf16[128,1024]{1,0:T(8,128)(2,1)S(1)}, u32[]{:S(2)}, u32[]{:S(2)}) collective-permute-start(bf16[128,1024]{1,0:T(8,128)(2,1)S(1)} %get-tuple-element.15), channel_id=1, source_target_pairs={{1,0},{2,1},{3,2},{4,3},{5,4},{6,5},{7,6},{8,7},{9,8},{10,9},{11,1... | collective-permute-start | bytes 786440 | tf_op jit(solution)/shard_map/ppermute | solution.py:22
  22.4 3.0 %collective-permute-done = bf16[128,1024]{1,0:T(8,128)(2,1)S(1)} collective-permute-done((bf16[128,1024]{1,0:T(8,128)(2,1)S(1)}, bf16[128,1024]{1,0:T(8,128)(2,1)S(1)}, u32[]{:S(2)}, u32[]{:S(2)}) %collective-permute-start) | collective-permute-done | bytes 262176 | tf_op jit(solution)/shard_map/ppermute | solution.py:19
  25.7 32.0 %all-gather.9.cloned.1.call-done = bf16[1024,1024]{1,0:T(8,128)(2,1)} async-done(((bf16[64,1024]{1,0:T(8,128)(2,1)}), bf16[1024,1024]{1,0:T(8,128)(2,1)}) %all-gather.9.cloned.1.call-update) | async-done | bytes 2097168 | tf_op jit(solution)/shard_map/all_gather | solution.py:101
  57.7 2.8 %convolution_convert_fusion.1 = bf16[512,1024]{1,0:T(8,128)(2,1)S(1)} fusion(bf16[1024,1024]{1,0:T(8,128)(2,1)} %all-gather.9.cloned.1.call-done, bf16[128,1024]{1,0:T(8,128)(2,1)S(1)} %collective-permute-done.1, bf16[256,1024]{1,0:T(8,128)(2,1)S(1)} %fusion.9, bf16[128,1024]{1,0:T(8,128)(2,1)S(1)} %collective-permute-done), kind=kOutput, calls=%fused_computation.34 | convolution fusion | flops 1077411840 | bytes 4194304 | tf_op jit(solution)/shard_map/dot_general | solution.py:107
  64.5 35.5 %all-gather.11.cloned.1.call-done = bf16[1024,1024]{1,0:T(8,128)(2,1)} async-done(((bf16[64,1024]{1,0:T(8,128)(2,1)}), bf16[1024,1024]{1,0:T(8,128)(2,1)}) %all-gather.11.cloned.1.call-update) | async-done | bytes 2097168 | tf_op jit(solution)/shard_map/all_gather | solution.py:102
  100.0 3.0 %convolution_convert_fusion = bf16[512,1024]{1,0:T(8,128)(2,1)S(1)} fusion(bf16[1024,1024]{1,0:T(8,128)(2,1)} %all-gather.11.cloned.1.call-done, bf16[128,1024]{1,0:T(8,128)(2,1)} %copy-done.22, bf16[256,1024]{1,0:T(8,128)(2,1)S(1)} %fusion.9, bf16[128,1024]{1,0:T(8,128)(2,1)} %copy-done.21), kind=kOutput, calls=%fused_computation.33 | convolution fusion | flops 1077411840 | bytes 4194304 | tf_op jit(solution)/shard_map/dot_general | solution.py:108
  130.8 11.6 %all-gather.7.cloned.1.call-done = bf16[1024,1024]{1,0:T(8,128)(2,1)} async-done(((bf16[64,1024]{1,0:T(8,128)(2,1)}), bf16[1024,1024]{1,0:T(8,128)(2,1)}) %all-gather.7.cloned.1.call-update) | async-done | bytes 2097168 | tf_op jit(solution)/shard_map/all_gather | solution.py:100
  144.9 4.5 %convert_multiply_fusion = (f32[256,1024]{1,0:T(8,128)}, f32[256,1024]{1,0:T(8,128)S(1)}, f32[256,1024]{1,0:T(8,128)}, f32[256,1024]{1,0:T(8,128)}, f32[256,1024...) fusion(bf16[256,1024]{1,0:T(8,128)(2,1)S(1)} %convolution_convert_fusion.2, ...), kind=kLoop, calls=%fused_computation.21 | loop fusion | flops 4456448 | bytes 13107200 | tf_op jit(solution)/shard_map/mul | solution.py:51
  149.4 2.6 copy.55
  152.0 2.6 copy.57
  154.6 2.6 copy.59
  157.1 2.6 copy.61
  159.7 2.6 copy.63
  186.6 2.6 copy.62
  190.2 2.6 copy.64
  193.9 2.6 copy.66
  197.5 2.6 copy.67
  200.1 6.5 %fusion.1 = bf16[256,1024]{1,0:T(8,128)(2,1)S(1)} fusion(bf16[1024,1024]{1,0:T(8,128)(2,1)} %all-gather.13.cloned.1.call-done, bf16[256,1024]{1,0:T(8,128)(2,1)S(1)} %copy-done.1, f32[256,1024]{1,0:T(8,128)} %copy.67, f32[256,1024]{1,0:T(8,128)} %copy.66, bf16[256,1024]{1,0:T(8,128)(2,1)} %gather_fusion.16, f32[256,1024]{1,0:T(8,128)} %copy.64, ...), kind=kOutput, calls=%fused_computation.35 | convolution fusion | flops 544210944 | bytes 16777216 | tf_op jit(solution)/shard_map/dot_general | solution.py:114
  206.6 4.3 %gather_fusion.17 = bf16[1024,1024]{1,0:T(8,128)(2,1)S(1)} fusion(bf16[256,1024]{1,0:T(8,128)(2,1)S(1)} %fusion.1, s32[1024]{0:T(1024)S(1)} %broadcast_clamp_fusion.2), kind=kCustom, calls=%fused_computation.17 | custom fusion | bytes 4198400 | tf_op jit(solution)/shard_map/gather | solution.py:63
  210.9 5.3 %gather_fusion.18 = bf16[1024,1024]{1,0:T(8,128)(2,1)} fusion(bf16[256,1024]{1,0:T(8,128)(2,1)S(1)} %fusion.1, s32[1024]{0:T(1024)S(1)} %broadcast_clamp_fusion.1), kind=kCustom, calls=%fused_computation.18 | custom fusion | bytes 4198400 | tf_op jit(solution)/shard_map/gather | solution.py:63
  216.2 5.3 %gather_fusion.19 = bf16[1024,1024]{1,0:T(8,128)(2,1)} fusion(bf16[256,1024]{1,0:T(8,128)(2,1)S(1)} %fusion.1, s32[1024]{0:T(1024)S(1)} %broadcast_clamp_fusion), kind=kCustom, calls=%fused_computation.19 | custom fusion | bytes 4198400 | tf_op jit(solution)/shard_map/gather | solution.py:63
  221.5 3.7 %fusion.4 = bf16[1024,100]{0,1:T(8,128)(2,1)S(1)} fusion(bf16[100,1024]{1,0:T(8,128)(2,1)S(1)} %copy-done, bf16[1024,1024]{1,0:T(8,128)(2,1)} %gather_fusion.19, bf16[1024,1024]{1,0:T(8,128)(2,1)} %gather_fusion.18, bf16[1024,1024]{1,0:T(8,128)(2,1)S(1)} %gather_fusion.17, f32[1024]{0:T(1024)S(1)} %bitcast.121, f32[1024]{0:T(1024)S(1)} %bitcast.122, ...), kind=kOutput, calls=%fused_computation.39 | convolution fusion | flops 219254784 | bytes 6713344 | tf_op jit(solution)/shard_map/dot_general | solution.py:66
  225.2 8.3 %all-gather.1 = bf16[2,100,1024]{2,1,0:T(8,128)(2,1)S(1)} all-gather(bf16[1,100,1024]{2,1,0:T(8,128)(2,1)S(1)} %bitcast.108), channel_id=2, replica_groups=mesh['member'=2,'space'=16] {'member'}, dimensions={0}, use_global_device_ids=true | all-gather | bytes 614400 | tf_op jit(solution)/shard_map/all_gather | solution.py:122
  235.9 38.3 %psum.7 = f32[]{:T(128)} all-reduce(f32[]{:T(128)} %multiply_reduce_fusion), channel_id=1, replica_groups=mesh['member'=2,'space'=16] {'member','space'}, use_global_device_ids=true, to_apply=%region_13.0 | all-reduce | flops 1 | bytes 8 | tf_op jit(solution)/shard_map/psum | solution.py:146
  (128 shorter events, 74.0 us)
Async XLA Ops:
  7.2 214.4 %copy-start = (bf16[100,1024]{1,0:T(8,128)(2,1)S(1)}, bf16[100,1024]{1,0:T(8,128)(2,1)}, u32[]{:S(2)}) copy-start(bf16[100,1024]{1,0:T(8,128)(2,1)} %param.27) | copy-start | bytes 614404
  7.2 6.8 %copy-start.1 = (bf16[256,1024]{1,0:T(8,128)(2,1)S(1)}, bf16[256,1024]{1,0:T(8,128)(2,1)}, u32[]{:S(2)}) copy-start(bf16[256,1024]{1,0:T(8,128)(2,1)} %param.15) | copy-start | bytes 1572868
  7.2 6.8 %copy-start.20 = (f32[1024]{0:T(1024)S(1)}, f32[1024]{0:T(1024)}, u32[]{:S(2)}) copy-start(f32[1024]{0:T(1024)} %param.17) | copy-start | bytes 12292
  7.2 50.5 %all-gather.9.cloned.1.call-start = ((), (), s32[]{:S(2)}) async-start(), calls=%async_computation.1 | async-start | bytes 2228224 | tf_op jit(solution)/shard_map/all_gather | solution.py:101
  7.9 92.1 %all-gather.11.cloned.1.call-start = ((), (), s32[]{:S(2)}) async-start(), calls=%async_computation.2 | async-start | bytes 2228224 | tf_op jit(solution)/shard_map/all_gather | solution.py:102
  8.7 133.7 %all-gather.7.cloned.1.call-start = ((), (), s32[]{:S(2)}) async-start(), calls=%async_computation | async-start | bytes 2228224 | tf_op jit(solution)/shard_map/all_gather | solution.py:100
  9.4 190.7 %all-gather.13.cloned.1.call-start = ((), (), s32[]{:S(2)}) async-start(), calls=%async_computation.3 | async-start | bytes 2228224 | tf_op jit(solution)/shard_map/all_gather | solution.py:113
  14.4 6.9 %copy-start.19 = (s32[8,256]{1,0:T(8,128)S(1)}, s32[8,256]{1,0:T(8,128)}, u32[]{:S(2)}) copy-start(s32[8,256]{1,0:T(8,128)} %param.23) | copy-start | bytes 24580
  14.4 7.0 %copy-start.13 = (bf16[100,1024]{1,0:T(8,128)(2,1)S(1)}, bf16[100,1024]{1,0:T(8,128)(2,1)}, u32[]{:S(2)}) copy-start(bf16[100,1024]{1,0:T(8,128)(2,1)} %param.28) | copy-start | bytes 614404
  15.6 6.6 %copy-start.17 = (s32[3,1024]{1,0:T(4,128)S(1)}, s32[3,1024]{1,0:T(4,128)}, u32[]{:S(2)}) copy-start(s32[3,1024]{1,0:T(4,128)} %param.25) | copy-start | bytes 36868
  15.6 6.7 %copy-start.16 = (f32[1024]{0:T(1024)S(1)}, f32[1024]{0:T(1024)}, u32[]{:S(2)}) copy-start(f32[1024]{0:T(1024)} %param.29) | copy-start | bytes 12292
  15.6 6.7 %copy-start.18 = (f32[3,1024]{1,0:T(4,128)S(1)}, f32[3,1024]{1,0:T(4,128)}, u32[]{:S(2)}) copy-start(f32[3,1024]{1,0:T(4,128)} %param.26) | copy-start | bytes 36868
  15.7 9.7 %collective-permute-start = (bf16[128,1024]{1,0:T(8,128)(2,1)S(1)}, bf16[128,1024]{1,0:T(8,128)(2,1)S(1)}, u32[]{:S(2)}, u32[]{:S(2)}) collective-permute-start(bf16[128,1024]{1,0:T(8,128)(2,1)S(1)} %get-tuple-element.14), channel_id=1, source_target_pairs={{0,1},{1,2},{2,3},{3,4},{4,5},{5,6},{6,7},{7,8},{8,9},{9,10},{10,1... | collective-permute-start | bytes 786440 | tf_op jit(solution)/shard_map/ppermute | solution.py:19
  16.2 9.4 %collective-permute-start.1 = (bf16[128,1024]{1,0:T(8,128)(2,1)S(1)}, bf16[128,1024]{1,0:T(8,128)(2,1)S(1)}, u32[]{:S(2)}, u32[]{:S(2)}) collective-permute-start(bf16[128,1024]{1,0:T(8,128)(2,1)S(1)} %get-tuple-element.15), channel_id=1, source_target_pairs={{1,0},{2,1},{3,2},{4,3},{5,4},{6,5},{7,6},{8,7},{9,8},{10,9},{11,1... | collective-permute-start | bytes 786440 | tf_op jit(solution)/shard_map/ppermute | solution.py:22
  25.4 35.1 %copy-start.21 = (bf16[128,1024]{1,0:T(8,128)(2,1)}, bf16[128,1024]{1,0:T(8,128)(2,1)S(1)}, u32[]{:S(2)}) copy-start(bf16[128,1024]{1,0:T(8,128)(2,1)S(1)} %collective-permute-done) | copy-start | bytes 786436
  25.7 34.9 %copy-start.22 = (bf16[128,1024]{1,0:T(8,128)(2,1)}, bf16[128,1024]{1,0:T(8,128)(2,1)S(1)}, u32[]{:S(2)}) copy-start(bf16[128,1024]{1,0:T(8,128)(2,1)S(1)} %collective-permute-done.1) | copy-start | bytes 786436
  130.8 14.1 %copy-start.7 = (bf16[256,1024]{1,0:T(8,128)(2,1)S(1)}, bf16[256,1024]{1,0:T(8,128)(2,1)}, u32[]{:S(2)}) copy-start(bf16[256,1024]{1,0:T(8,128)(2,1)} %gather_fusion.11) | copy-start | bytes 1572868
  142.4 2.5 copy-start.10
  142.4 2.5 copy-start.11
  142.4 2.5 copy-start.12
  166.1 3.3 %copy-start.4 = (f32[256,1024]{0,1:T(8,128)S(1)}, f32[256,1024]{0,1:T(8,128)}, u32[]{:S(2)}) copy-start(f32[256,1024]{0,1:T(8,128)} %copy.59) | copy-start | bytes 3145732
  167.5 3.6 %copy-start.3 = (f32[256,1024]{0,1:T(8,128)S(1)}, f32[256,1024]{0,1:T(8,128)}, u32[]{:S(2)}) copy-start(f32[256,1024]{0,1:T(8,128)} %copy.63) | copy-start | bytes 3145732
  167.5 3.6 %copy-start.5 = (f32[256,1024]{0,1:T(8,128)S(1)}, f32[256,1024]{0,1:T(8,128)}, u32[]{:S(2)}) copy-start(f32[256,1024]{0,1:T(8,128)} %copy.65) | copy-start | bytes 3145732
  225.2 8.4 %copy-start.15 = (f32[100,512]{1,0:T(8,128)S(1)}, f32[100,512]{1,0:T(8,128)}, u32[]{:S(2)}) copy-start(f32[100,512]{1,0:T(8,128)} %constant_dynamic-slice_fusion) | copy-start | bytes 614404
  (5 other events, 10.1 us)
Sparse Core Ops, SparseCore 0:
  10.2 47.4 all-gather.8
  59.8 40.1 all-gather.10
  102.2 40.1 all-gather.6
  144.4 40.1 all-gather.12
where the time goes:
time: 284 us; the launch traced here: 282 us
  local copies, waits for them, and re-layouts  95.2 us (34%)
  waiting for transfers between devices  84.6 us (30%)
  blocking collectives  46.6 us (16%)
  matrix products  19.8 us (7%)
  between operations  16.1 us (6%)
  other arithmetic  14.5 us (5%)
  starting transfers between devices  5.75 us (2%)
    psum x1, blocking collectives, per_device(): loss_sum = lax.psum(local_sum, ('member', 'space'))  38.3 us
    all_gather x1, waiting for transfers between devices, per_device(): lax.all_gather(w_value, 'space', axis=0, tiled=True)  35.5 us
    all_gather x1, waiting for transfers between devices, per_device(): lax.all_gather(w_key, 'space', axis=0, tiled=True)  32 us
    mul x16, local copies, waits for them, and re-layouts, attention(): numerator = numerator + weight[:, :, None] * gathered_value  24.8 us
    mul x8, local copies, waits for them, and re-layouts, attention(): weight = jnp.exp(jnp.sum(query_wide * gathered_key, axis=2) * factor)  18 us
    gather x8, local copies, waits for them, and re-layouts, attention(): key_ext[picked].astype(jnp.float32).reshape(row_count, HEADS, head_size)  15.9 us
    gather x8, local copies, waits for them, and re-layouts, attention(): value_ext[picked].astype(jnp.float32).reshape(row_count, HEADS, head_size)  15.8 us
    gather x3, local copies, waits for them, and re-layouts, decode(): processed[sources[neighbour]].astype(jnp.float32)  14.9 us
  transfers between devices with their start and end apart: 6, of which 5 were waited for; matrix products, arithmetic and copies ran while one was open for 36% of the time, Pallas kernels for 0%

commit v1 on v0

v1 whole, which is shorter than its diff:
```python
import functools
import math

import jax
import jax.numpy as jnp
from jax import lax
from jax.experimental import pallas as pl
from jax.experimental.pallas import tpu as pltpu
from jax.sharding import PartitionSpec as P

HEADS = 16
SMOOTH = 0.25
EPS = 1e-05
BF = jnp.bfloat16
F32 = jnp.float32
AXES = ("member", "space")
NT = (((1,), (1,)), ((), ()))
TN = (((0,), (0,)), ((), ()))
NONE = -1e30


def dot(a, b, dims=(((1,), (0,)), ((), ()))):
    return lax.dot_general(a, b, dims, preferred_element_type=F32)


def round_up(value, unit):
    return -(-value // unit) * unit


def chip_cycle(chips):
    rows = 1
    while rows * rows * 4 <= chips:
        rows *= 2
    if rows == 1 and chips > 2:
        rows = 2
    depth = chips // rows
    if rows * depth != chips or rows == 1:
        return list(range(chips))
    walk = []
    for y in range(rows):
        zs = range(1, depth) if y % 2 == 0 else range(depth - 1, 0, -1)
        walk += [z * rows + y for z in zs]
    return walk + [y for y in range(rows - 1, -1, -1)]


class Links:
    def __init__(self, members, space):
        self.members, self.space = members, space
        self.chips = space // 2
        self.cycle = chip_cycle(self.chips)
        self.place = [0] * self.chips
        for at, chip in enumerate(self.cycle):
            self.place[chip] = at

    def pairs(self, target):
        out = []
        for m in range(self.members):
            for s in range(self.space):
                tm, ts = target(m, s)
                out.append((m * self.space + s, tm * self.space + ts))
        return out

    def ring(self):
        def target(m, s):
            chip, core = divmod(s, 2)
            step = 1 if core == 0 else -1
            return m, 2 * self.cycle[(self.place[chip] + step) % self.chips] + core

        return self.pairs(target)

    def partner(self):
        return self.pairs(lambda m, s: (m, s ^ 1))

    def outer_halo(self):
        return self.pairs(lambda m, s: (m, (s + (1 if s % 2 else -1)) % self.space))

    def member_shift(self, shift):
        return self.pairs(lambda m, s: ((m - shift) % self.members, s))

    def space_flip(self, bit):
        return self.pairs(lambda m, s: (m, s ^ bit))

    def member_flip(self, bit):
        return self.pairs(lambda m, s: (m ^ bit, s))


def send(x, pairs):
    return lax.ppermute(x, AXES, pairs)


VM = pl.BlockSpec(memory_space=pltpu.VMEM)
SM = pl.BlockSpec(memory_space=pltpu.SMEM)
ANY = pl.BlockSpec(memory_space=pl.ANY)


def start_kernel(where, wq, wk, wv, wo, wd, states, noise, rows, pack, outer, inner):
    m, c = where[0], where[1]
    width = pack.shape[1] - wide(wd.shape[0])
    third = width // 3
    mine = pl.ds(pl.multiple_of(m * third, 128), third)
    for at, ref in enumerate((wq, wk, wv)):
        pack[:, at * third : (at + 1) * third] = ref[:, mine]
    folded = dot(wo[...], wd[...], NT)
    pad = wide(wd.shape[0]) - wd.shape[0]
    folded = jnp.concatenate([folded, jnp.zeros((folded.shape[0], pad), F32)], axis=1)
    pack[:, width:] = folded.astype(BF)
    halo = rows.shape[1] // 2
    nodes = states.shape[0]
    numbers = lax.broadcasted_iota(jnp.int32, (nodes, halo), 0)
    low, high = rows[:, :halo], rows[:, halo:]
    for ref, first in ((outer, c == 0), (inner, c != 0)):
        picked = jnp.where(first, low, high)
        chosen = (numbers == picked).astype(F32).astype(BF)
        if ref.shape[1] == states.shape[1]:
            source = states[...]
        else:
            source = states[:, pl.ds(pl.multiple_of(m * ref.shape[1], 128), ref.shape[1])]
        ref[:halo, :] = dot(chosen, source, TN).astype(BF)
        terms = dot(noise[...], chosen).astype(BF)
        if ref.shape[1] > halo:
            rest = jnp.zeros((terms.shape[0], ref.shape[1] - halo), BF)
            terms = jnp.concatenate([terms, rest], axis=1)
        ref[halo:, :] = terms


def wide(count):
    return round_up(count, 128)


def prepare_kernel(where, edges, states, wd, sources, weights, bias, base, upper, lower):
    c = where[1]
    nodes = states.shape[0]
    total = bias.shape[1]
    halo = (total - nodes) // 2
    e = edges[...]
    turned = jnp.where(e < halo, e + (nodes + halo), jnp.where(e >= nodes + halo, e - (nodes + halo), e))
    e = jnp.where(c == 0, e, turned)
    numbers = lax.broadcasted_iota(jnp.int32, (total, nodes), 0)
    count = jnp.zeros((total, nodes), F32)
    for k in range(e.shape[0]):
        count = count + (numbers == e[k : k + 1, :]).astype(F32)
    logs = jnp.where(count > 0, jnp.log2(jnp.maximum(count, 1.0)), NONE)
    bias[...] = logs.T
    fields = dot(wd[...], states[...], NT)
    pad = base.shape[0] - fields.shape[0]
    base[...] = jnp.concatenate([fields, jnp.zeros((pad, nodes), F32)], axis=0)
    grid = sources.shape[1]
    step = min(grid, 512)
    for at in range(0, grid, step):
        cut = slice(at, at + step)
        numbers = lax.broadcasted_iota(jnp.int32, (nodes, step), 0)
        matrix = jnp.zeros((nodes, step), F32)
        for k in range(sources.shape[0]):
            hit = numbers == sources[k : k + 1, cut]
            matrix = matrix + jnp.where(hit, weights[k : k + 1, cut], 0.0)
        high = matrix.astype(BF)
        upper[:, cut] = high
        lower[:, cut] = (matrix - high.astype(F32)).astype(BF)


def hidden_kernel(where, states, outer, crossed, inner, noise, gain, cond, hidden, values):
    m = where[0]
    members = hidden.shape[0]
    nodes = states.shape[0]
    halo = (hidden.shape[1] - nodes) // 2
    part = outer.shape[1]
    for k in range(members):
        owner = lax.rem(m + k, members)
        source = outer[:halo, :] if k == 0 else crossed[k - 1]
        values[:halo, pl.ds(pl.multiple_of(owner * part, 128), part)] = source.astype(F32)
    values[halo : halo + nodes, :] = states[...].astype(F32)
    values[halo + nodes :, :] = inner[:halo, :].astype(F32)
    width = states.shape[1]
    for at in range(0, hidden.shape[1], 128):
        cut = slice(at, at + 128)
        x = values[cut, :]
        center = x - jnp.mean(x, axis=1, keepdims=True)
        spread = jnp.mean(center * center, axis=1, keepdims=True)
        normed = center * lax.rsqrt(spread + EPS) * gain[...]
        for k in range(members):
            terms = dot(noise[k, :, cut], cond[...], TN)
            hidden[k, cut, :] = (normed * (1.0 + terms[:, :width]) + terms[:, width:]).astype(BF)


def attend_kernel(halves, where, places, hidden, bias, *rest):
    pieces = rest[: len(halves)]
    out, weights, attended, sems = rest[len(halves) :]
    m = where[0]
    step = pl.program_id(0)
    rows = pieces[0].shape[0] // halves[0]

    def copies():
        at = 0
        for ref, count in zip(pieces, halves):
            for half in range(count):
                row = pl.multiple_of(places[at] * rows, rows)
                yield pltpu.make_async_copy(
                    ref.at[pl.ds(half * rows, rows), :], weights.at[pl.ds(row, rows), :], sems.at[at]
                )
                at += 1

    @pl.when(step == 0)
    def _():
        for copy in copies():
            copy.start()
        for copy in copies():
            copy.wait()

    nodes = bias.shape[0]
    total = hidden.shape[1]
    halo = (total - nodes) // 2
    model = hidden.shape[2]
    head = model // HEADS
    third = attended.shape[1]
    scale = math.log2(math.e) / math.sqrt(head)
    every = hidden[0]
    own = hidden[0, halo : halo + nodes, :]
    query = (dot(own, weights[:, :third]) * scale).astype(BF)
    key = dot(every, weights[:, third : 2 * third]).astype(BF)
    value = dot(every, weights[:, 2 * third : 3 * third]).astype(BF)
    group = 128
    lanes = lax.broadcasted_iota(jnp.int32, (nodes, group), 1)
    ones = jnp.ones((total, 128), BF)
    for at in range(0, third, group):
        cut = slice(at, at + group)
        q, k = query[:, cut], key[:, cut]
        v = jnp.concatenate([value[:, cut], ones], axis=1)
        result = None
        for first in range(0, group, head):
            inside = (lanes >= first) & (lanes < first + head)
            masked = jnp.where(inside, q, jnp.zeros_like(q))
            scores = dot(masked, k, NT) + bias[...]
            both = dot(jnp.exp2(scores).astype(BF), v)
            normal = both[:, :group] / both[:, group:]
            result = normal if result is None else jnp.where(inside, normal, result)
        attended[:, cut] = result.astype(BF)
    mine = weights[pl.ds(pl.multiple_of(m * third, 128), third), 3 * third :]
    partial = dot(attended[...], mine)
    out[0] = partial.T[: out.shape[1], :].astype(BF)


def score_kernel(own, others, base, upper, lower, truth, area, grads, loss):
    members, _, _ = own.shape
    variables, grid = truth.shape
    fields = []
    for k in range(members):
        total = own[k].astype(F32)
        for j in range(members - 1):
            total = total + others[j, (k - (j + 1)) % members].astype(F32)
        total = total + base[...]
        high = total.astype(BF)
        low = (total - high.astype(F32)).astype(BF)
        x = dot(high, upper[...]) + (dot(low, upper[...]) + dot(high, lower[...]))
        fields.append(x[:variables].astype(BF).astype(F32))
    y = truth[...].astype(F32)
    weight = area[...]

    def both(d):
        square = d * d + SMOOTH * SMOOTH
        inverse = lax.rsqrt(square)
        return square * inverse, d * inverse

    skill = spread = None
    for k in range(members):
        size, slope = both(fields[k] - y)
        skill = size if skill is None else skill + size
        if k == 0:
            gradient = slope
    pull = None
    for k in range(members):
        for j in range(k + 1, members):
            size, slope = both(fields[k] - fields[j])
            spread = size if spread is None else spread + size
            if k == 0:
                pull = slope if pull is None else pull + slope
    gradient = gradient - pull * (1.0 / (members - 1))
    grads[0] = (weight * gradient).astype(BF)
    crps = skill * (1.0 / members) - spread * (1.0 / (members * (members - 1)))
    summed = jnp.sum(jnp.sum(weight * crps, axis=0, keepdims=True), axis=1, keepdims=True)
    loss[...] = jnp.broadcast_to(summed, loss.shape)


def params(megabytes=32):
    return pltpu.CompilerParams(vmem_limit_bytes=megabytes << 20)


def per_device(
    links,
    node_states,
    noise,
    norm_gain,
    cond_weight,
    w_query,
    w_key,
    w_value,
    w_out,
    edge_src,
    send_rows,
    dec_src,
    dec_weight,
    w_decode,
    truth,
    area,
):
    shape = jax.ShapeDtypeStruct
    members, space = links.members, links.space
    m, s = lax.axis_index("member"), lax.axis_index("space")
    chip, core = s // 2, s % 2
    nodes, model = node_states.shape
    rows = w_query.shape[0]
    third = model // members
    variables, grid = truth.shape
    halo = send_rows.shape[0] // 2
    total = nodes + 2 * halo
    channels = noise.shape[1]
    packed = 3 * third + wide(variables)
    tall = round_up(variables, 16)
    where = jnp.stack([m, core]).astype(jnp.int32)
    own_noise = noise[0]

    shard, outer_out, inner_out = pl.pallas_call(
        start_kernel,
        out_shape=(
            shape((rows, packed), BF),
            shape((halo + channels, third), BF),
            shape((halo + channels, model), BF),
        ),
        in_specs=[SM] + [VM] * 8,
        out_specs=(VM, VM, VM),
        compiler_params=params(),
        name="start",
    )(where, w_query, w_key, w_value, w_out, w_decode, node_states, own_noise, send_rows[None, :])

    partner, ring = links.partner(), links.ring()
    other = send(shard, partner)
    place = jnp.asarray(links.place, jnp.int32)[chip]
    cycle = jnp.asarray(links.cycle, jnp.int32)
    turn = jnp.where(core == 0, -1, 1)
    pieces, halves, order = [shard, other], [1, 1], [s, s ^ 1]
    current = jnp.concatenate([shard, other], axis=0)
    rounds = links.chips // 2
    for r in range(1, rounds + 1):
        last = r == rounds and links.chips % 2 == 0
        current = send(current[:rows] if last else current, ring)
        passed = send(current, partner)
        near = 2 * cycle[(place + turn * r) % links.chips]
        far = 2 * cycle[(place - turn * r) % links.chips]
        pieces += [current, passed]
        if last:
            halves += [1, 1]
            order += [near + core, far + 1 - core]
        else:
            halves += [2, 2]
            order += [near + core, near + 1 - core, far + 1 - core, far + core]

    outer_in = send(outer_out, links.outer_halo())
    inner_in = send(inner_out, partner)
    terms = jnp.concatenate([outer_in[halo:, :halo], own_noise, inner_in[halo:, :halo]], axis=1)
    if third == total:
        message = jnp.concatenate([outer_in[:halo], terms], axis=0)
        crossed = [send(message, links.member_shift(k)) for k in range(1, members)]
        crossed_states = jnp.stack([x[:halo] for x in crossed])
        crossed_terms = [x[halo:] for x in crossed]
    else:
        crossed_states = jnp.stack(
            [send(outer_in[:halo], links.member_shift(k)) for k in range(1, members)]
        )
        crossed_terms = [send(terms, links.member_shift(k)) for k in range(1, members)]
    all_terms = jnp.stack([terms] + crossed_terms)

    bias, base, upper, lower = pl.pallas_call(
        prepare_kernel,
        out_shape=(
            shape((nodes, total), F32),
            shape((tall, nodes), F32),
            shape((nodes, grid), BF),
            shape((nodes, grid), BF),
        ),
        in_specs=[SM] + [VM] * 5,
        out_specs=(VM,) * 4,
        compiler_params=params(),
        name="prepare",
    )(where, edge_src, node_states, w_decode, dec_src, dec_weight)

    hidden = pl.pallas_call(
        hidden_kernel,
        out_shape=shape((members, total, model), BF),
        in_specs=[SM] + [VM] * 7,
        out_specs=VM,
        scratch_shapes=[pltpu.VMEM((total, model), F32)],
        compiler_params=params(),
        name="hidden",
    )(where, node_states, outer_in, crossed_states, inner_in, all_terms, norm_gain[None, :], cond_weight)

    partial = pl.pallas_call(
        functools.partial(attend_kernel, tuple(halves)),
        out_shape=shape((members, tall, nodes), BF),
        grid_spec=pltpu.PrefetchScalarGridSpec(
            num_scalar_prefetch=2,
            grid=(members,),
            in_specs=[
                pl.BlockSpec((1, total, model), lambda i, *_: (i, 0, 0)),
                pl.BlockSpec((nodes, total), lambda i, *_: (0, 0)),
            ]
            + [ANY] * len(pieces),
            out_specs=pl.BlockSpec((1, tall, nodes), lambda i, *_: (i, 0, 0)),
            scratch_shapes=[
                pltpu.VMEM((model, packed), BF),
                pltpu.VMEM((nodes, third), BF),
                pltpu.SemaphoreType.DMA((sum(halves),)),
            ],
        ),
        compiler_params=params(),
        name="attend",
    )(where, jnp.stack(order).astype(jnp.int32), hidden, bias, *pieces)

    others = jnp.stack([send(partial, links.member_shift(k)) for k in range(1, members)])
    field_grad, loss = pl.pallas_call(
        score_kernel,
        out_shape=(shape((1, variables, grid), BF), shape((8, 128), F32)),
        in_specs=[VM] * 7,
        out_specs=(VM, VM),
        compiler_params=params(),
        name="score",
    )(partial, others, base, upper, lower, truth, area[None, :])

    bit = 1
    while bit < space:
        loss = loss + send(loss, links.space_flip(bit))
        bit *= 2
    if members > 2:
        bit = 1
        while bit < members:
            loss = loss + send(loss, links.member_flip(bit))
            bit *= 2
        loss = loss * (1.0 / members)
    loss = loss[0, 0] / (variables * grid * space)
    return (loss, field_grad)


def solution(mesh):
    in_specs = (
        P("space", None),
        P("member", None, "space"),
        P(),
        P(),
        P("space", None),
        P("space", None),
        P("space", None),
        P("space", None),
        P(None, "space"),
        P("space"),
        P(None, "space"),
        P(None, "space"),
        P(),
        P(None, "space"),
        P("space"),
    )
    out_specs = (P(), P("member", None, "space"))
    links = Links(mesh.shape["member"], mesh.shape["space"])
    return jax.shard_map(
        functools.partial(per_device, links),
        mesh=mesh,
        in_specs=in_specs,
        out_specs=out_specs,
        check_vma=False,
    )
```

time: 284 us -> 101 us (0.36)
  local copies, waits for them, and re-layouts: 95.2 us -> 13.3 us
  blocking collectives: 46.6 us -> 0 us
  waiting for transfers between devices: 84.6 us -> 42.9 us
  matrix products: 19.8 us -> 0 us
  Pallas kernels: 0 us -> 17.3 us
  other arithmetic: 14.5 us -> 0.81 us
  starting transfers between devices: 5.75 us -> 12.9 us
    all_gather x4 -> x0, waiting for transfers between devices: 79.2 us -> none  [the longest x1 35.5 us: per_device(): lax.all_gather(w_value, 'space', axis=0, tiled=True)]
    gather x20 -> x0, local copies, waits for them, and re-layouts: 47.7 us -> none  [the longest x8 15.9 us: attention(): key_ext[picked].astype(jnp.float32).reshape(row_count, HEADS, head_size)]
    mul x24 -> x0, local copies, waits for them, and re-layouts: 42.9 us -> none  [the longest x16 24.8 us: attention(): numerator = numerator + weight[:, :, None] * gathered_value]
    ppermute x2 -> x17, waiting for transfers between devices: 3.3 us -> 42.9 us  [send(): return lax.ppermute(x, AXES, pairs)]
    psum x1 -> x0, blocking collectives: 38.3 us -> none  [per_device(): loss_sum = lax.psum(local_sum, ('member', 'space'))]
    dot_general x6 -> x0, matrix products: 19.8 us -> none  [the longest x1 6.49 us: per_device(): update = jnp.dot(attended, whole_out, preferred_element_type=jnp.float32)]
    pallas_call x0 -> x5, Pallas kernels: none -> 17.3 us  [the longest x1 10.9 us: per_device(): pl.pallas_call(functools.partial(attend_kernel, tuple(halves)), out_shape...]
    unnamed x46 -> x48, local copies, waits for them, and re-layouts: 0.15 us -> 9.68 us
  transfers between devices with their start and end apart: 6 -> 17, of which waited for: 5 -> 10; matrix products, arithmetic and copies ran while one was open for 36% -> 4% of each run, Pallas kernels for 0% -> 4%
where the time goes in v1:
time: 101 us; the launch traced here: 100 us
  waiting for transfers between devices  42.9 us (42%)
  Pallas kernels  17.3 us (17%)
  local copies, waits for them, and re-layouts  13.3 us (13%)
  between operations  13.3 us (13%)
  starting transfers between devices  12.9 us (13%)
    ppermute x17, waiting for transfers between devices, send(): return lax.ppermute(x, AXES, pairs)  42.9 us
    ppermute x17, starting transfers between devices, send(): return lax.ppermute(x, AXES, pairs)  12.9 us
    pallas_call x1, Pallas kernels, per_device(): pl.pallas_call(functools.partial(attend_kernel, tuple(halves)), out_shape...  10.9 us
    unnamed x48, local copies, waits for them, and re-layouts  9.68 us
    pallas_call x1, Pallas kernels, per_device(): pl.pallas_call(hidden_kernel, out_shape=shape((members, total, model), BF...  2.08 us
  transfers between devices with their start and end apart: 17, of which 10 were waited for; matrix products, arithmetic and copies ran while one was open for 4% of the time, Pallas kernels for 4%

profile of v1, /device:TPU:0, one launch (start us, length us, event | category | flops | bytes accessed | tf_op | source)
XLA Modules:
  0.0 100.4 jit_solution(8607740057924056321)
XLA Ops:
  0.8 1.0 %copy-done = bf16[256,1024]{1,0:T(8,128)(2,1)S(1)} copy-done((bf16[256,1024]{1,0:T(8,128)(2,1)S(1)}, bf16[256,1024]{1,0:T(8,128)(2,1)}, u32[]{:S(2)}) %copy-start) | copy-done | bytes 524312
  1.8 0.9 copy-done.2
  7.8 0.9 start.1
  9.3 1.1 %collective-permute-done.3.rest_1_ = bf16[64,1664]{1,0:T(8,128)(2,1)S(1)} collective-permute-done((bf16[64,1664]{1,0:T(8,128)(2,1)S(1)}, bf16[64,1664]{1,0:T(8,128)(2,1)S(1)}, u32[]{:S(2)}, u32[]{:S(2)}) %collective-permute-start.3) | collective-permute-done | bytes 213024 | tf_op jit(solution)/shard_map/ppermute | solution.py:88
  10.4 3.0 %collective-permute-start.4 = (bf16[128,1664]{1,0:T(8,128)(2,1)S(1)}, bf16[128,1664]{1,0:T(8,128)(2,1)S(1)}, u32[]{:S(2)}, u32[]{:S(2)}) collective-permute-start(bf16[128,1664]{1,0:T(8,128)(2,1)S(1)} %pad_maximum_fusion), channel_id=1, source_target_pairs={{0,4},{1,3},{2,0},{3,7},{4,8},{5,1},{6,2},{7,11},{8,12},{9,5},{10,... | collective-permute-start | bytes 1277960 | tf_op jit(solution)/shard_map/ppermute | solution.py:88
  13.4 6.0 %collective-permute-done.4.rest_2_ = bf16[128,1664]{1,0:T(8,128)(2,1)S(1)} collective-permute-done((bf16[128,1664]{1,0:T(8,128)(2,1)S(1)}, bf16[128,1664]{1,0:T(8,128)(2,1)S(1)}, u32[]{:S(2)}, u32[]{:S(2)}) %collective-permute-start.4) | collective-permute-done | bytes 426016 | tf_op jit(solution)/shard_map/ppermute | solution.py:88
  19.4 2.1 %collective-permute-start.6 = (bf16[128,1664]{1,0:T(8,128)(2,1)S(1)}, bf16[128,1664]{1,0:T(8,128)(2,1)}, u32[]{:S(2)}, u32[]{:S(2)}) collective-permute-start(bf16[128,1664]{1,0:T(8,128)(2,1)S(1)} %collective-permute-done.4.rest_2_), channel_id=1, source_target_pairs={{0,4},{1,3},{2,0},{3,7},{4,8},{5,1},{6,2},{7,11},{8,12},{9,5},{10,... | collective-permute-start | bytes 1277960 | tf_op jit(solution)/shard_map/ppermute | solution.py:88
  21.5 6.1 %collective-permute-done.6.rest_4_ = bf16[128,1664]{1,0:T(8,128)(2,1)} collective-permute-done((bf16[128,1664]{1,0:T(8,128)(2,1)S(1)}, bf16[128,1664]{1,0:T(8,128)(2,1)}, u32[]{:S(2)}, u32[]{:S(2)}) %collective-permute-start.6) | collective-permute-done | bytes 426016 | tf_op jit(solution)/shard_map/ppermute | solution.py:88
  27.7 2.1 %collective-permute-start.8 = (bf16[128,1664]{1,0:T(8,128)(2,1)}, bf16[128,1664]{1,0:T(8,128)(2,1)S(1)}, u32[]{:S(2)}, u32[]{:S(2)}) collective-permute-start(bf16[128,1664]{1,0:T(8,128)(2,1)} %collective-permute-done.6.rest_4_), channel_id=1, source_target_pairs={{0,4},{1,3},{2,0},{3,7},{4,8},{5,1},{6,2},{7,11},{8,12},{9,5},{10,... | collective-permute-start | bytes 1277960 | tf_op jit(solution)/shard_map/ppermute | solution.py:88
  29.8 1.2 %collective-permute-start = (bf16[144,512]{1,0:T(8,128)(2,1)S(1)}, bf16[144,512]{1,0:T(8,128)(2,1)S(1)}, u32[]{:S(2)}, u32[]{:S(2)}) collective-permute-start(bf16[144,512]{1,0:T(8,128)(2,1)S(1)} %get-tuple-element.11), channel_id=1, source_target_pairs={{0,15},{1,2},{2,1},{3,4},{4,3},{5,6},{6,5},{7,8},{8,7},{9,10},{10,... | collective-permute-start | bytes 442376 | tf_op jit(solution)/shard_map/ppermute | solution.py:88
  31.0 7.6 %collective-permute-done.outer = bf16[144,512]{1,0:T(8,128)(2,1)S(1)} collective-permute-done((bf16[144,512]{1,0:T(8,128)(2,1)S(1)}, bf16[144,512]{1,0:T(8,128)(2,1)S(1)}, u32[]{:S(2)}, u32[]{:S(2)}) %collective-permute-start) | collective-permute-done | bytes 147488 | tf_op jit(solution)/shard_map/ppermute | solution.py:88
  40.0 1.5 %collective-permute-start.2 = (bf16[144,512]{1,0:T(8,128)(2,1)}, bf16[144,512]{1,0:T(8,128)(2,1)}, u32[]{:S(2)}, u32[]{:S(2)}) collective-permute-start(bf16[144,512]{1,0:T(8,128)(2,1)} %maximum_maximum_fusion), channel_id=1, source_target_pairs={{0,16},{1,17},{2,18},{3,19},{4,20},{5,21},{6,22},{7,23},{8,24},{9,... | collective-permute-start | bytes 442376 | tf_op jit(solution)/shard_map/ppermute | solution.py:88
  53.5 1.7 %prepare.1 = (f32[256,512]{1,0:T(8,128)S(1)}, f32[112,256]{1,0:T(8,128)S(1)}, bf16[256,1024]{1,0:T(8,128)(2,1)S(1)}, bf16[256,1024]{1,0:T(8,128)(2,1)S(1)}) custom-call(s32[2]{0:T(128)S(1)} %pad_add_fusion.where, s32[8,256]{1,0:T(8,128)S(1)} %copy-done.18, bf16[256,1024]{1,0:T(8,128)(2,1)S(1)} %copy-done.1, bf16[100,1024]{1,0:T(8,128)(2,1)S(1)} %copy-done.3, ...), custom_call_target="tpu_custom_call" | custom-call | tf_op jit(solution)/shard_map/prepare/pallas_call | solution.py:371
  57.4 4.6 %collective-permute-done.10.rest_8_ = bf16[64,1664]{1,0:T(8,128)(2,1)S(1)} collective-permute-done((bf16[64,1664]{1,0:T(8,128)(2,1)S(1)}, bf16[64,1664]{1,0:T(8,128)(2,1)S(1)}, u32[]{:S(2)}, u32[]{:S(2)}) %collective-permute-start.10) | collective-permute-done | bytes 213024 | tf_op jit(solution)/shard_map/ppermute | solution.py:88
  62.9 1.0 copy-done.7
  63.9 2.1 %hidden.1 = bf16[2,512,1024]{2,1,0:T(8,128)(2,1)S(1)} custom-call(s32[2]{0:T(128)S(1)} %pad_add_fusion.where, bf16[256,1024]{1,0:T(8,128)(2,1)S(1)} %copy-done.1, bf16[144,512]{1,0:T(8,128)(2,1)S(1)} %collective-permute-done.outer, bf16[1,128,512]{2,1,0:T(8,128)(2,1)S(1)} %slice_bitcast_fusion.crossed, bf16[144,1024]{1,0:T(8,128)(2,1)S(1)} %copy-done.7, ...), custom_call_target="tpu_custom_call" | custom-call | tf_op jit(solution)/shard_map/hidden/pallas_call | solution.py:385
  66.0 1.0 copy-done.5
  67.0 10.9 %attend.1.own = bf16[2,112,256]{2,1,0:T(8,128)(2,1)S(1)} custom-call(s32[2]{0:T(128)S(1)} %pad_add_fusion.where, s32[16]{0:T(128)S(1)} %stack.94.places, bf16[2,512,1024]{2,1,0:T(8,128)(2,1)S(1)} %hidden.1, f32[256,512]{1,0:T(8,128)S(1)} %get-tuple-element.13.bias, bf16[64,1664]{1,0:T(8,128)(2,1)S(1)} %get-tuple-element.14.rest_0_, ...), custom_call_target="tpu_custom_call" | custom-call | tf_op jit(solution)/shard_map/attend/pallas_call | solution.py:395
  78.4 5.2 %collective-permute-done.12 = bf16[2,112,256]{2,1,0:T(8,128)(2,1)S(1)} collective-permute-done((bf16[2,112,256]{2,1,0:T(8,128)(2,1)S(1)}, bf16[2,112,256]{2,1,0:T(8,128)(2,1)S(1)}, u32[]{:S(2)}, u32[]{:S(2)}) %collective-permute-start.12) | collective-permute-done | bytes 114720 | tf_op jit(solution)/shard_map/ppermute | solution.py:88
  83.6 1.7 %score.1 = (bf16[1,100,1024]{2,1,0:T(8,128)(2,1)}, f32[8,128]{1,0:T(8,128)S(1)}) custom-call(bf16[2,112,256]{2,1,0:T(8,128)(2,1)S(1)} %attend.1.own, bf16[1,2,112,256]{3,2,1,0:T(8,128)(2,1)S(1)} %bitcast.39, f32[112,256]{1,0:T(8,128)S(1)} %get-tuple-element.15.base, bf16[256,1024]{1,0:T(8,128)(2,1)S(1)} %get-tuple-element.16.upper, ...), custom_call_target="tpu_custom_call" | custom-call | tf_op jit(solution)/shard_map/score/pallas_call | solution.py:418
  85.2 1.2 %collective-permute-done.13 = f32[8,128]{1,0:T(8,128)S(1)} collective-permute-done((f32[8,128]{1,0:T(8,128)S(1)}, f32[8,128]{1,0:T(8,128)S(1)}, u32[]{:S(2)}, u32[]{:S(2)}) %collective-permute-start.13) | collective-permute-done | bytes 4128 | tf_op jit(solution)/shard_map/ppermute | solution.py:88
  86.8 3.2 %collective-permute-done.14 = f32[8,128]{1,0:T(8,128)S(1)} collective-permute-done((f32[8,128]{1,0:T(8,128)S(1)}, f32[8,128]{1,0:T(8,128)S(1)}, u32[]{:S(2)}, u32[]{:S(2)}) %collective-permute-start.14) | collective-permute-done | bytes 4128 | tf_op jit(solution)/shard_map/ppermute | solution.py:88
  90.0 3.6 %collective-permute-done.15 = f32[8,128]{1,0:T(8,128)S(1)} collective-permute-done((f32[8,128]{1,0:T(8,128)S(1)}, f32[8,128]{1,0:T(8,128)S(1)}, u32[]{:S(2)}, u32[]{:S(2)}) %collective-permute-start.15) | collective-permute-done | bytes 4128 | tf_op jit(solution)/shard_map/ppermute | solution.py:88
  93.9 4.2 %collective-permute-done.16 = f32[8,128]{1,0:T(8,128)S(1)} collective-permute-done((f32[8,128]{1,0:T(8,128)S(1)}, f32[8,128]{1,0:T(8,128)S(1)}, u32[]{:S(2)}, u32[]{:S(2)}) %collective-permute-start.16) | collective-permute-done | bytes 4128 | tf_op jit(solution)/shard_map/ppermute | solution.py:88
  (82 shorter events, 13.3 us)
Async XLA Ops:
  0.6 47.2 %copy-start.22 = (s32[8]{0:T(128)S(1)}, s32[8]{0:T(128)}, u32[]{:S(2)}) copy-start(s32[8]{0:T(128)} %constant.98.clone) | copy-start | bytes 100
  0.7 52.8 %copy-start.17 = (f32[3,1024]{1,0:T(4,128)S(1)}, f32[3,1024]{1,0:T(4,128)}, u32[]{:S(2)}) copy-start(f32[3,1024]{1,0:T(4,128)} %weights.1) | copy-start | bytes 36868
  0.7 52.8 %copy-start.16 = (s32[3,1024]{1,0:T(4,128)S(1)}, s32[3,1024]{1,0:T(4,128)}, u32[]{:S(2)}) copy-start(s32[3,1024]{1,0:T(4,128)} %sources.1) | copy-start | bytes 36868
  7.8 45.7 %copy-start.3 = (bf16[100,1024]{1,0:T(8,128)(2,1)S(1)}, bf16[100,1024]{1,0:T(8,128)(2,1)}, u32[]{:S(2)}) copy-start(bf16[100,1024]{1,0:T(8,128)(2,1)} %wd.3) | copy-start | bytes 614404
  7.8 45.8 %copy-start.18 = (s32[8,256]{1,0:T(8,128)S(1)}, s32[8,256]{1,0:T(8,128)}, u32[]{:S(2)}) copy-start(s32[8,256]{1,0:T(8,128)} %edges.1) | copy-start | bytes 24580
  7.8 55.1 %copy-start.15 = (bf16[16,2048]{1,0:T(8,128)(2,1)S(1)}, bf16[16,2048]{1,0:T(8,128)(2,1)}, u32[]{:S(2)}) copy-start(bf16[16,2048]{1,0:T(8,128)(2,1)} %cond.1) | copy-start | bytes 196612
  7.8 55.2 %copy-start.19 = (f32[1024]{0:T(1024)S(1)}, f32[1024]{0:T(1024)}, u32[]{:S(2)}) copy-start(f32[1024]{0:T(1024)} %param.19) | copy-start | bytes 12292
  8.7 1.7 %collective-permute-start.3 = (bf16[64,1664]{1,0:T(8,128)(2,1)S(1)}, bf16[64,1664]{1,0:T(8,128)(2,1)S(1)}, u32[]{:S(2)}, u32[]{:S(2)}) collective-permute-start(bf16[64,1664]{1,0:T(8,128)(2,1)S(1)} %get-tuple-element.14.rest_0_), channel_id=1, source_target_pairs={{0,1},{1,0},{2,3},{3,2},{4,5},{5,4},{6,7},{7,6},{8,9},{9,8},{10,11... | collective-permute-start | bytes 638984 | tf_op jit(solution)/shard_map/ppermute | solution.py:88
  10.4 9.0 %collective-permute-start.4 = (bf16[128,1664]{1,0:T(8,128)(2,1)S(1)}, bf16[128,1664]{1,0:T(8,128)(2,1)S(1)}, u32[]{:S(2)}, u32[]{:S(2)}) collective-permute-start(bf16[128,1664]{1,0:T(8,128)(2,1)S(1)} %pad_maximum_fusion), channel_id=1, source_target_pairs={{0,4},{1,3},{2,0},{3,7},{4,8},{5,1},{6,2},{7,11},{8,12},{9,5},{10,... | collective-permute-start | bytes 1277960 | tf_op jit(solution)/shard_map/ppermute | solution.py:88
  19.4 8.2 %collective-permute-start.6 = (bf16[128,1664]{1,0:T(8,128)(2,1)S(1)}, bf16[128,1664]{1,0:T(8,128)(2,1)}, u32[]{:S(2)}, u32[]{:S(2)}) collective-permute-start(bf16[128,1664]{1,0:T(8,128)(2,1)S(1)} %collective-permute-done.4.rest_2_), channel_id=1, source_target_pairs={{0,4},{1,3},{2,0},{3,7},{4,8},{5,1},{6,2},{7,11},{8,12},{9,5},{10,... | collective-permute-start | bytes 1277960 | tf_op jit(solution)/shard_map/ppermute | solution.py:88
  21.5 17.1 %collective-permute-start.1 = (bf16[144,1024]{1,0:T(8,128)(2,1)S(1)}, bf16[144,1024]{1,0:T(8,128)(2,1)S(1)}, u32[]{:S(2)}, u32[]{:S(2)}) collective-permute-start(bf16[144,1024]{1,0:T(8,128)(2,1)S(1)} %get-tuple-element.12), channel_id=1, source_target_pairs={{0,1},{1,0},{2,3},{3,2},{4,5},{5,4},{6,7},{7,6},{8,9},{9,8},{10,11... | collective-permute-start | bytes 884744 | tf_op jit(solution)/shard_map/ppermute | solution.py:88
  27.7 28.4 %collective-permute-start.8 = (bf16[128,1664]{1,0:T(8,128)(2,1)}, bf16[128,1664]{1,0:T(8,128)(2,1)S(1)}, u32[]{:S(2)}, u32[]{:S(2)}) collective-permute-start(bf16[128,1664]{1,0:T(8,128)(2,1)} %collective-permute-done.6.rest_4_), channel_id=1, source_target_pairs={{0,4},{1,3},{2,0},{3,7},{4,8},{5,1},{6,2},{7,11},{8,12},{9,5},{10,... | collective-permute-start | bytes 1277960 | tf_op jit(solution)/shard_map/ppermute | solution.py:88
  29.8 8.8 %collective-permute-start = (bf16[144,512]{1,0:T(8,128)(2,1)S(1)}, bf16[144,512]{1,0:T(8,128)(2,1)S(1)}, u32[]{:S(2)}, u32[]{:S(2)}) collective-permute-start(bf16[144,512]{1,0:T(8,128)(2,1)S(1)} %get-tuple-element.11), channel_id=1, source_target_pairs={{0,15},{1,2},{2,1},{3,4},{4,3},{5,6},{6,5},{7,8},{8,7},{9,10},{10,... | collective-permute-start | bytes 442376 | tf_op jit(solution)/shard_map/ppermute | solution.py:88
  40.0 16.6 %collective-permute-start.2 = (bf16[144,512]{1,0:T(8,128)(2,1)}, bf16[144,512]{1,0:T(8,128)(2,1)}, u32[]{:S(2)}, u32[]{:S(2)}) collective-permute-start(bf16[144,512]{1,0:T(8,128)(2,1)} %maximum_maximum_fusion), channel_id=1, source_target_pairs={{0,16},{1,17},{2,18},{3,19},{4,20},{5,21},{6,22},{7,23},{8,24},{9,... | collective-permute-start | bytes 442376 | tf_op jit(solution)/shard_map/ppermute | solution.py:88
  55.3 10.7 %collective-permute-start.5 = (bf16[128,1664]{1,0:T(8,128)(2,1)}, bf16[128,1664]{1,0:T(8,128)(2,1)S(1)}, u32[]{:S(2)}, u32[]{:S(2)}) collective-permute-start(bf16[128,1664]{1,0:T(8,128)(2,1)} %copy-done.4), channel_id=1, source_target_pairs={{0,1},{1,0},{2,3},{3,2},{4,5},{5,4},{6,7},{7,6},{8,9},{9,8},{10,11... | collective-permute-start | bytes 1277960 | tf_op jit(solution)/shard_map/ppermute | solution.py:88
  56.0 10.0 %collective-permute-start.7 = (bf16[128,1664]{1,0:T(8,128)(2,1)}, bf16[128,1664]{1,0:T(8,128)(2,1)S(1)}, u32[]{:S(2)}, u32[]{:S(2)}) collective-permute-start(bf16[128,1664]{1,0:T(8,128)(2,1)} %collective-permute-done.6.rest_4_), channel_id=1, source_target_pairs={{0,1},{1,0},{2,3},{3,2},{4,5},{5,4},{6,7},{7,6},{8,9},{9,8},{10,11... | collective-permute-start | bytes 1277960 | tf_op jit(solution)/shard_map/ppermute | solution.py:88
  56.1 5.9 %collective-permute-start.10 = (bf16[64,1664]{1,0:T(8,128)(2,1)S(1)}, bf16[64,1664]{1,0:T(8,128)(2,1)S(1)}, u32[]{:S(2)}, u32[]{:S(2)}) collective-permute-start(bf16[64,1664]{1,0:T(8,128)(2,1)S(1)} %slice.33), channel_id=1, source_target_pairs={{0,4},{1,3},{2,0},{3,7},{4,8},{5,1},{6,2},{7,11},{8,12},{9,5},{10,... | collective-permute-start | bytes 638984 | tf_op jit(solution)/shard_map/ppermute | solution.py:88
  56.1 9.9 %collective-permute-start.9 = (bf16[128,1664]{1,0:T(8,128)(2,1)S(1)}, bf16[128,1664]{1,0:T(8,128)(2,1)S(1)}, u32[]{:S(2)}, u32[]{:S(2)}) collective-permute-start(bf16[128,1664]{1,0:T(8,128)(2,1)S(1)} %collective-permute-done.8.rest_6_), channel_id=1, source_target_pairs={{0,1},{1,0},{2,3},{3,2},{4,5},{5,4},{6,7},{7,6},{8,9},{9,8},{10,11... | collective-permute-start | bytes 1277960 | tf_op jit(solution)/shard_map/ppermute | solution.py:88
  62.0 4.0 %collective-permute-start.11 = (bf16[64,1664]{1,0:T(8,128)(2,1)S(1)}, bf16[64,1664]{1,0:T(8,128)(2,1)S(1)}, u32[]{:S(2)}, u32[]{:S(2)}) collective-permute-start(bf16[64,1664]{1,0:T(8,128)(2,1)S(1)} %collective-permute-done.10.rest_8_), channel_id=1, source_target_pairs={{0,1},{1,0},{2,3},{3,2},{4,5},{5,4},{6,7},{7,6},{8,9},{9,8},{10,11... | collective-permute-start | bytes 638984 | tf_op jit(solution)/shard_map/ppermute | solution.py:88
  77.9 5.6 %collective-permute-start.12 = (bf16[2,112,256]{2,1,0:T(8,128)(2,1)S(1)}, bf16[2,112,256]{2,1,0:T(8,128)(2,1)S(1)}, u32[]{:S(2)}, u32[]{:S(2)}) collective-permute-start(bf16[2,112,256]{2,1,0:T(8,128)(2,1)S(1)} %attend.1.own), channel_id=1, source_target_pairs={{0,16},{1,17},{2,18},{3,19},{4,20},{5,21},{6,22},{7,23},{8,24},{9,... | collective-permute-start | bytes 344072 | tf_op jit(solution)/shard_map/ppermute | solution.py:88
  85.2 1.2 %collective-permute-start.13 = (f32[8,128]{1,0:T(8,128)S(1)}, f32[8,128]{1,0:T(8,128)S(1)}, u32[]{:S(2)}, u32[]{:S(2)}) collective-permute-start(f32[8,128]{1,0:T(8,128)S(1)} %get-tuple-element.18), channel_id=1, source_target_pairs={{0,1},{1,0},{2,3},{3,2},{4,5},{5,4},{6,7},{7,6},{8,9},{9,8},{10,11... | collective-permute-start | bytes 12296 | tf_op jit(solution)/shard_map/ppermute | solution.py:88
  86.4 3.6 %collective-permute-start.14 = (f32[8,128]{1,0:T(8,128)S(1)}, f32[8,128]{1,0:T(8,128)S(1)}, u32[]{:S(2)}, u32[]{:S(2)}) collective-permute-start(f32[8,128]{1,0:T(8,128)S(1)} %add.162), channel_id=1, source_target_pairs={{0,2},{1,3},{2,0},{3,1},{4,6},{5,7},{6,4},{7,5},{8,10},{9,11},{10,... | collective-permute-start | bytes 12296 | tf_op jit(solution)/shard_map/ppermute | solution.py:88
  90.0 3.6 %collective-permute-start.15 = (f32[8,128]{1,0:T(8,128)S(1)}, f32[8,128]{1,0:T(8,128)S(1)}, u32[]{:S(2)}, u32[]{:S(2)}) collective-permute-start(f32[8,128]{1,0:T(8,128)S(1)} %add.163), channel_id=1, source_target_pairs={{0,4},{1,5},{2,6},{3,7},{4,0},{5,1},{6,2},{7,3},{8,12},{9,13},{10,... | collective-permute-start | bytes 12296 | tf_op jit(solution)/shard_map/ppermute | solution.py:88
  93.6 4.5 %collective-permute-start.16 = (f32[8,128]{1,0:T(8,128)S(1)}, f32[8,128]{1,0:T(8,128)S(1)}, u32[]{:S(2)}, u32[]{:S(2)}) collective-permute-start(f32[8,128]{1,0:T(8,128)S(1)} %add.164), channel_id=1, source_target_pairs={{0,8},{1,9},{2,10},{3,11},{4,12},{5,13},{6,14},{7,15},{8,0},{9,1},... | collective-permute-start | bytes 12296 | tf_op jit(solution)/shard_map/ppermute | solution.py:88
  (17 other events, 170.2 us)
